TPU v7x, 256 devices: a whole 4x4x8 slice. The times are simulated.
256 devices in a mesh: row: 16 (over y_lo, x, core), team: 16 (over y_hi, z).
Axes of the slice: x: 4, y: 4 (y_hi: 2, y_lo: 2; y = y_hi * 2 + y_lo), z: 8, core: 2. Of those that a mesh axis runs over, the one named last changes fastest.
Arguments:
- features: bfloat16 [32768, 512], P('row'), may hold values from -6 to 6
- weight: bfloat16 [512, 512], replicated, may hold values from -0.25 to 0.25
- table: bfloat16 [8, 512], replicated, may hold values from -5 to 5
- labels: int32 [32768], P('row'), may hold values from 0 to 7
- label_mask: int32 [32768], P('row'), may hold values 0 or 1
- block_vals: bfloat16 [16, 16, 16, 128, 128], P('row', 'team'), may hold values from -0.25 to 0.25
- block_row: int32 [16, 16, 16], P('row', 'team'), may hold values from 0 to 15, as said below
- block_col: int32 [16, 16, 16], P('row', 'team'), may hold values from 0 to 15
- block_count: int32 [16, 16], P('row', 'team'), may hold values from 1 to 16, as said below
Outputs:
- output: bfloat16 [32768, 512], P(('row', 'team'))
- grad_weight: float32 [512, 512], replicated
- grad_features: bfloat16 [16, 2048, 512], P('team', 'row')
Inputs may be any that keep to these rules, and one draw needn't show every extreme that they name: Within one [r, t] list the pairs (block_row, block_col) of all 16 slots are distinct. Only the first block_count[r, t] slots of a list are live; some [r, t] has exactly 16 live slots in every draw.
All inputs are finite; a program needn't handle non-finite values. No bound on the sum of `label_mask` on one device may be relied on, other than what follows from the above.
Results may differ from a plain program's by a relative error of at most 0.0059.
Values may be sent and summed in bfloat16 or wider, within the bound.
A program may use at most 64 MiB of HBM per device.

v0:
```python
import math

import jax
import jax.numpy as jnp
from jax import lax
from jax.sharding import PartitionSpec as P


def spread_2(value, axis, source):
    kept = jnp.where(lax.axis_index(axis) == source, value, 0).astype(value.dtype)
    return lax.psum(kept, axis)


def silu_slope(preact):
    sigma = jax.nn.sigmoid(preact)
    return sigma * (1.0 + preact * (1.0 - sigma))


def block_product(sources, values, gather_ids, target_ids, live_count, out_blocks, form):
    total_slots = values.shape[0]
    group_size = min(32, total_slots)
    feature_width = sources.shape[1]
    source_blocks = sources.reshape(sources.shape[0] // 128, 128, feature_width)
    target_table = jnp.arange(out_blocks, dtype=jnp.int32)

    def add_group(group_index, totals):
        first_slot = group_index * group_size
        group_values = values
        live_slots = first_slot + jnp.arange(group_size, dtype=jnp.int32) < live_count
        group_values = jnp.where(
            live_slots[:, None, None], group_values, jnp.zeros_like(group_values)
        )
        picked = source_blocks[gather_ids]
        product = jnp.einsum(form, group_values, picked, preferred_element_type=jnp.float32)
        upper = product.astype(jnp.bfloat16)
        upper_wide = lax.optimization_barrier(upper).astype(jnp.float32)
        lower = (product - upper_wide).astype(jnp.bfloat16)
        selector = (target_ids[None, :] == target_table[:, None]).astype(jnp.bfloat16)
        folded = jnp.einsum("sk,kif->sif", selector, upper, preferred_element_type=jnp.float32)
        folded = folded + jnp.einsum(
            "sk,kif->sif", selector, lower, preferred_element_type=jnp.float32
        )
        return totals + folded

    groups = (live_count + group_size - 1) // group_size
    totals = lax.fori_loop(
        jnp.int32(0), groups, add_group, jnp.zeros((out_blocks, 128, feature_width), jnp.float32)
    )
    return totals.reshape(out_blocks * 128, feature_width)


def local_layer(agg, weight, table, labels, label_mask):
    preact = jnp.dot(agg, weight, preferred_element_type=jnp.float32)
    active = jax.nn.silu(preact)
    classes = jnp.arange(table.shape[0], dtype=jnp.int32)
    onehot = (labels[:, None] == classes[None, :]).astype(jnp.float32)
    target = jnp.dot(onehot, table.astype(jnp.float32), precision=lax.Precision.HIGHEST)
    residual = label_mask.astype(jnp.float32)[:, None] * (active - target)
    grad_pre = (residual * silu_slope(preact)).astype(jnp.bfloat16)
    back_rows = jnp.dot(grad_pre, weight.T, preferred_element_type=jnp.float32).astype(jnp.bfloat16)
    return (active.astype(jnp.bfloat16), grad_pre, back_rows)


def per_device(
    features, weight, table, labels, label_mask, block_vals, block_row, block_col, block_count
):
    slab_rows = features.shape[0]
    row_count = lax.axis_size("row")
    team_count = lax.axis_size("team")
    sections = row_count // team_count
    team_index = lax.axis_index("team")
    share_rows = slab_rows // team_count
    share_start = team_index * share_rows
    slab_blocks = slab_rows // 128
    values = block_vals[0, 0]
    row_ids = block_row[0, 0]
    col_ids = block_col[0, 0]
    live_count = block_count[0, 0]
    pieces = spread_2(features, "row", team_index * sections + 0)
    partial_value = block_product(
        pieces, values, col_ids, row_ids, live_count, slab_blocks, "kij,kjf->kif"
    )
    summed = lax.psum(partial_value, "team")
    agg = summed.astype(jnp.bfloat16)
    output_full, grad_pre, back_rows = local_layer(agg, weight, table, labels, label_mask)
    agg_share = lax.dynamic_slice_in_dim(agg, share_start, share_rows, 0)
    grad_share = lax.dynamic_slice_in_dim(grad_pre, share_start, share_rows, 0)
    output = lax.dynamic_slice_in_dim(output_full, share_start, share_rows, 0)
    weight_term = jnp.dot(agg_share.T, grad_share, preferred_element_type=jnp.float32)
    grad_weight = lax.psum(weight_term, ("row", "team")) * (1.0 / math.sqrt(slab_rows * row_count))
    spread = block_product(
        back_rows, values, row_ids, col_ids, live_count, sections * slab_blocks, "kji,kjf->kif"
    )
    grad_piece = lax.psum_scatter(spread, "row", scatter_dimension=0, tiled=True).astype(
        jnp.bfloat16
    )
    return (output, grad_weight, grad_piece[None])


def solution(mesh):
    placed = (
        P("row", None),
        P(),
        P(),
        P("row"),
        P("row"),
        P("row", "team", None, None, None),
        P("row", "team", None),
        P("row", "team", None),
        P("row", "team"),
    )
    return jax.shard_map(
        per_device,
        mesh=mesh,
        in_specs=placed,
        out_specs=(P(("row", "team"), None), P(), P("team", "row", None)),
        check_vma=False,
    )
```

profile of v0, /device:TPU:1, one launch (start us, length us, event | category | flops | bytes accessed | tf_op | source)
XLA Modules:
  0.0 608.1 jit_solution(13963354870653102805)
XLA Ops:
  7.2 1.5 broadcast_select_fusion
  9.8 1.0 copy.23
  10.8 131.9 %all-reduce.4.cloned.1.call-done = bf16[16,128,512]{2,1,0:T(8,128)(2,1)} async-done(((bf16[16,128,512]{2,1,0:T(8,128)(2,1)}), bf16[16,128,512]{2,1,0:T(8,128)(2,1)}) %all-reduce.4.cloned.1.call-update) | async-done | bytes 2097168 | tf_op jit(solution)/shard_map/psum | solution.py:11
  142.8 2.3 gather_fusion
  145.0 2.5 broadcast.89.clone
  147.5 8.8 %while.26 = (s32[]{:T(128)}, f32[16,128,512]{2,0,1:T(8,128)}, s32[]{:T(128)}, s32[1,1,16]{2,1,0:T(1,128)S(1)}, s32[]{:T(128)}, /*index=5*/bf16[16,128,128]{2,1,0...) while((s32[]{:T(128)}, f32[16,128,512]{2,0,1:T(8,128)}, s32[]{:T(128)}, ...), condition=%wide.region_2.3_spmd.clone, body=%wide.region_1.2_spmd.clone.sunk | while | flops 342098464 | bytes 71827784 | solution.py:46
  148.2 0.7 fusion.66
  148.9 0.8 subtract_convert_fusion.4
  149.8 1.3 fusion.67
  151.1 0.8 copy-done.4
  151.9 2.4 add_add_fusion.4
  154.3 1.9 copy-done.5
  156.3 6.6 %copy.25 = f32[16,128,512]{2,1,0:T(8,128)} copy(f32[16,128,512]{2,0,1:T(8,128)} %get-tuple-element.213) | data formatting | bytes 8388608 | tf_op jit(solution)/shard_map/while | solution.py:46
  162.9 98.9 %all-reduce.7 = bf16[2048,512]{1,0:T(8,128)(2,1)S(1)} all-reduce(f32[2048,512]{1,0:T(8,128)} %bitcast.54), channel_id=1, replica_groups=mesh['row'=16,'team'=16] {'team'}, use_global_device_ids=true, to_apply=%region_3.4 | all-reduce | flops 1048576 | bytes 6291456 | tf_op jit(solution)/shard_map/psum | solution.py:83
  261.8 3.2 fusion.30
  265.0 3.4 multiply_convert_fusion
  268.4 2.6 convolution_convert_fusion
  271.1 1.3 fusion.32
  272.4 2.3 gather_fusion.1
  274.7 2.5 broadcast.89
  277.2 8.8 %while.27 = (s32[]{:T(128)}, f32[16,128,512]{2,0,1:T(8,128)}, s32[]{:T(128)}, s32[1,1,16]{2,1,0:T(1,128)S(1)}, s32[]{:T(128)}, /*index=5*/bf16[16,128,128]{1,2,0...) while((s32[]{:T(128)}, f32[16,128,512]{2,0,1:T(8,128)}, s32[]{:T(128)}, ...), condition=%wide.region_6.7_spmd.clone, body=%wide.region_5.6_spmd.clone.sunk | while | flops 342098464 | bytes 71827784 | solution.py:46
  278.6 0.8 subtract_convert_fusion.5
  279.5 1.3 fusion.74
  280.8 0.8 copy-done.2
  281.6 2.4 add_add_fusion.5
  284.0 1.9 copy-done.3
  286.0 6.6 %copy.26 = f32[16,128,512]{2,1,0:T(8,128)} copy(f32[16,128,512]{2,0,1:T(8,128)} %get-tuple-element.214) | data formatting | bytes 8388608 | tf_op jit(solution)/shard_map/while | solution.py:46
  292.6 1.6 dynamic-slice_convert_fusion
  294.3 236.1 %all-reduce.6.cloned.1.call-done = f32[512,512]{1,0:T(8,128)} async-done(((f32[512,512]{1,0:T(8,128)}), f32[512,512]{1,0:T(8,128)}) %all-reduce.6.cloned.1.call-update) | async-done | bytes 1048592 | tf_op jit(solution)/shard_map/psum | solution.py:90
  530.4 2.3 broadcast_multiply_fusion
  532.7 67.3 %reduce-scatter.2.cloned.1.call-done = f32[128,512]{1,0:T(8,128)} async-done(((f32[2048,512]{1,0:T(8,128)}), f32[128,512]{1,0:T(8,128)}) %reduce-scatter.2.cloned.1.call-update) | async-done | bytes 262160 | tf_op jit(solution)/shard_map/reduce_scatter | solution.py:94
  599.9 1.6 convert_bitcast_fusion
  (36 shorter events, 2.5 us)
Async XLA Ops:
  7.2 254.6 %copy-start = (bf16[512,512]{1,0:T(8,128)(2,1)S(1)}, bf16[512,512]{1,0:T(8,128)(2,1)}, u32[]{:S(2)}) copy-start(bf16[512,512]{1,0:T(8,128)(2,1)} %param.14) | copy-start | bytes 1572868
  7.2 135.6 %all-reduce.4.cloned.1.call-start = ((), (), s32[]{:S(2)}) async-start(), calls=%async_computation.1 | async-start | bytes 4194304 | tf_op jit(solution)/shard_map/psum | solution.py:11
  8.7 0.8 copy-start.10
  8.7 1.1 copy-start.6
  8.7 2.1 copy-start.9
  8.7 2.1 copy-start.8
  8.7 521.6 %all-reduce.6.cloned.1.call-start = ((), (), s32[]{:S(2)}) async-start(), calls=%async_computation.2 | async-start | bytes 2097152 | tf_op jit(solution)/shard_map/psum | solution.py:90
  149.7 2.2 copy-start.4
  154.3 2.0 copy-start.5
  261.8 3.2 copy-start.11
  261.8 3.2 copy-start.12
  272.4 327.5 %reduce-scatter.2.cloned.1.call-start = ((), (), s32[]{:S(2)}) async-start(), calls=%async_computation.3 | async-start | bytes 4456448 | tf_op jit(solution)/shard_map/reduce_scatter | solution.py:94
  274.7 2.5 copy-start.7
  279.4 2.2 copy-start.2
  284.0 2.0 copy-start.3
  292.6 309.0 %copy-start.1 = (bf16[512,512]{1,0:T(8,128)(2,1)S(1)}, bf16[512,512]{1,0:T(8,128)(2,1)}, u32[]{:S(2)}) copy-start(bf16[512,512]{1,0:T(8,128)(2,1)} %param.14) | copy-start | bytes 1572868
Sparse Core Ops, SparseCore 0:
  10.6 132.0 all-reduce.3
  272.5 257.8 all-reduce.5
  532.9 66.9 reduce-scatter.1
where the time goes:
time: 611 us; the launch traced here: 608 us
  waiting for transfers between devices  435 us (71%)
  blocking collectives  98.9 us (16%)
  local copies, waits for them, and re-layouts  31.2 us (5%)
  matrix products  19.5 us (3%)
  between operations  14.6 us (2%)
  other arithmetic  8.34 us (1%)
    psum x1, waiting for transfers between devices, per_device(): lax.psum(weight_term, ('row', 'team'))  236 us
    psum x1, waiting for transfers between devices, spread_2(): return lax.psum(kept, axis)  132 us
    psum x1, blocking collectives, per_device(): summed = lax.psum(partial_value, 'team')  98.9 us
    reduce_scatter x1, waiting for transfers between devices, per_device(): lax.psum_scatter(spread, 'row', scatter_dimension=0, tiled=True)  67.3 us
    while x2, local copies, waits for them, and re-layouts, block_product(): lax.fori_loop(jnp.int32(0), groups, add_group, jnp.zeros((out_blocks, 128...  13.2 us
  transfers between devices with their start and end apart: 3, of which 3 were waited for; matrix products, arithmetic and copies ran while one was open for 4% of the time, Pallas kernels for 0%

commit v1 on v0

v1 whole, which is shorter than its diff:
```python
import functools
import math

import jax
import jax.numpy as jnp
from jax import lax
from jax.experimental import pallas as pl
from jax.experimental.pallas import tpu as pltpu
from jax.sharding import PartitionSpec as P

MESH = pl.DeviceIdType.MESH
BF16 = jnp.bfloat16
F32 = jnp.float32
HALVES = 2
WIDE = 256
PIECE = 64
TREES = ((0, 11), (11, 10), (21, 11))
DEEPEST = 5


def rem(value, size):
    return lax.rem(value, jnp.int32(size))


def div(value, size):
    return lax.div(value, jnp.int32(size))


def remote(src, dst, send_sem, recv_sem, device):
    return pltpu.make_async_remote_copy(
        src_ref=src,
        dst_ref=dst,
        send_sem=send_sem,
        recv_sem=recv_sem,
        device_id=device,
        device_id_type=MESH,
    )


def pick(index, table):
    value = jnp.int32(table[0])
    for position, entry in enumerate(table[1:], 1):
        value = jnp.where(index == position, jnp.int32(entry), value)
    return value


def layer_kernel(
    feat,
    weight,
    table,
    labels,
    mask,
    vals,
    brow,
    bcol,
    bcnt,
    out,
    gw_out,
    gf_out,
    xv,
    vt,
    slots,
    part,
    zs,
    zr,
    ys,
    yr,
    keep,
    gath,
    gw32,
    gwb,
    g1r,
    g1t,
    g2r,
    g3,
    g4,
    sp,
    prx,
    chip,
    xs,
    xr,
    bs,
    br,
    bc_recv,
    bc_send,
    z_send,
    z_recv,
    y_send,
    y_recv,
    ag_send,
    ag_recv,
    gw_send,
    gw_recv,
    p_send,
    p_recv,
    x_send,
    x_recv,
    b_send,
    b_recv,
):
    row = lax.axis_index("row")
    team = lax.axis_index("team")
    core = rem(row, 2)
    x = rem(div(row, 2), 4)
    ylo = div(row, 8)
    z = rem(team, 8)
    yhi = div(team, 8)

    def at_row(new_y, new_x, new_core):
        return ((new_y * 4 + rem(new_x + 4, 4)) * 2 + new_core, team)

    def at_team(new_yhi, new_z):
        return (row, new_yhi * 8 + rem(new_z + 8, 8))

    partner = at_row(ylo, x, 1 - core)
    x_up, x_down = at_row(ylo, x + 1, core), at_row(ylo, x - 1, core)
    y_side = at_row(1 - ylo, x, core)
    z_up, z_down = at_team(yhi, z + 1), at_team(yhi, z - 1)
    y_far = at_team(1 - yhi, z)

    barrier = pltpu.get_barrier_semaphore()

    def greet(d, carry):
        pl.semaphore_signal(
            barrier, inc=1, device_id=(rem(row + d, 16), team), device_id_type=MESH
        )
        pl.semaphore_signal(
            barrier, inc=1, device_id=(row, rem(team + d, 16)), device_id_type=MESH
        )
        return carry

    lax.fori_loop(1, 16, greet, 0)

    root = team
    root_core = rem(root, 2)
    rx = rem(x - rem(div(root, 2), 4) + 4, 4)
    ry = rem(ylo + div(root, 8), 2)
    lead = core == root_core
    is_root = row == root
    pieces = feat.shape[0] // PIECE

    def landed(piece):
        return xv.at[div(piece, 2), pl.ds(pl.multiple_of(rem(piece, 2) * PIECE, PIECE), PIECE)]

    def stage(piece):
        return pltpu.make_async_copy(
            feat.at[pl.ds(pl.multiple_of(piece * PIECE, PIECE), PIECE)],
            landed(piece),
            bc_recv.at[piece],
        )

    @pl.when(is_root)
    def _():
        def begin(piece, carry):
            stage(piece).start()
            return carry

        lax.fori_loop(0, pieces, begin, 0)

    slots[16] = jnp.zeros((128, 512), F32)
    for k in range(16):
        vt[k] = vals[k].T

    pl.semaphore_wait(barrier, 30)

    low = ry == 0
    depths = (
        jnp.where(low, pick(rx, (0, 1, 2, 3)), pick(rx, (5, 2, 3, 4))),
        jnp.where(low, pick(rx, (0, 3, 2, 1)), pick(rx, (5, 4, 3, 2))),
        jnp.where(low, pick(rx, (0, 3, 4, 3)), pick(rx, (1, 2, 3, 2))),
    )
    ups = (
        (low & (rx < 3)) | (~low & (rx > 1)),
        None,
        ~low & (rx < 2),
    )
    downs = (
        None,
        (low & (rx != 1)) | (~low & (rx > 0)),
        ~low & (rx == 0),
    )
    sides = (
        low & ((rx == 1) | (rx == 2)),
        low & (rx == 3),
        (low & (rx == 0)) | (~low & (rx > 0)),
    )

    def hop(piece, way, device):
        ref = landed(piece)
        return remote(ref, ref, bc_send.at[way, piece], bc_recv.at[piece], device)

    def branches(tree):
        return (
            (0, ups[tree], x_up),
            (1, downs[tree], x_down),
            (2, sides[tree], y_side),
            (3, None if tree < 0 else jnp.bool_(True), partner),
        )

    @pl.when(lead)
    def _():
        def beat(tick, carry):
            for tree, (first, number) in enumerate(TREES):
                q = tick - depths[tree]

                @pl.when((q >= 0) & (q < number))
                def _(tree=tree, first=first, q=q):
                    piece = first + q

                    @pl.when(is_root)
                    def _():
                        stage(piece).wait()

                    @pl.when(jnp.logical_not(is_root))
                    def _():
                        hop(piece, 3, partner).wait_recv()

                    for way, condition, device in branches(tree):
                        if condition is None:
                            continue

                        @pl.when(condition)
                        def _(way=way, device=device):
                            hop(piece, way, device).start()

            return carry

        lax.fori_loop(0, 11 + DEEPEST, beat, 0)

        def settle(q, carry):
            for tree, (first, number) in enumerate(TREES):

                @pl.when(q < number)
                def _(tree=tree, first=first):
                    for way, condition, device in branches(tree):
                        if condition is None:
                            continue

                        @pl.when(condition)
                        def _(way=way, device=device):
                            hop(first + q, way, device).wait_send()

            return carry

        lax.fori_loop(0, 11, settle, 0)

    @pl.when(jnp.logical_not(lead))
    def _():
        def arrive(piece, carry):
            hop(piece, 3, partner).wait_recv()
            return carry

        lax.fori_loop(0, pieces, arrive, 0)

    count = bcnt[0]

    def before(ids, k):
        found = jnp.int32(16)
        for other in range(k):
            found = jnp.where(ids[other] == ids[k], jnp.int32(other), found)
        return found

    def final(ids, target):
        found = jnp.int32(16)
        for other in range(16):
            hit = (ids[other] == target) & (jnp.int32(other) < count)
            found = jnp.where(hit, jnp.int32(other), found)
        return found

    for k in range(16):
        product = jnp.dot(vals[k], xv[bcol[k]], preferred_element_type=F32)
        slots[k] = product + slots[before(brow, k)] if k else product
    for s in range(16):
        value = slots[final(brow, s)].astype(BF16)
        for h in range(HALVES):
            part[h, s] = value[:, h * WIDE : (h + 1) * WIDE]

    def block(new_z, rel):
        return rem(yhi + rel, 2) * 8 + rem(new_z + 8, 8)

    ways = ((0, 1, z_up), (1, -1, z_down))

    def z_first(h, way, sign, device):
        return remote(
            part.at[h, block(z + 4, way)],
            zr.at[way, 0, h, way],
            z_send.at[way, 0, h],
            z_recv.at[way, 0, h],
            device,
        )

    def z_hop(h, way, step, device):
        return remote(
            zs.at[way, step, h],
            zr.at[way, step, h],
            z_send.at[way, step, h],
            z_recv.at[way, step, h],
            device,
        )

    for h in range(HALVES):
        for way, sign, device in ways:
            z_first(h, way, sign, device).start()
    for step in range(1, 4):
        for h in range(HALVES):
            for way, sign, device in ways:
                if step == 1:
                    z_first(h, way, sign, device).wait_recv()
                else:
                    z_hop(h, way, step - 1, device).wait_recv()
                for rel in range(2):
                    value = part[h, block(z + sign * (4 - step), rel)]
                    if step > 1 or rel == way:
                        value = (
                            value.astype(F32) + zr[way, step - 1, h, rel].astype(F32)
                        ).astype(BF16)
                    zs[way, step, h, rel] = value
                z_hop(h, way, step, device).start()

    def y_hop(h):
        return remote(ys.at[h], yr.at[h], y_send.at[h], y_recv.at[h], y_far)

    for h in range(HALVES):
        for way, sign, device in ways:
            z_hop(h, way, 3, device).wait_recv()
        sums = [
            part[h, block(z, rel)].astype(F32)
            + zr[0, 3, h, rel].astype(F32)
            + zr[1, 3, h, rel].astype(F32)
            for rel in range(2)
        ]
        ys[h] = sums[1].astype(BF16)
        y_hop(h).start()
        keep[:, h * WIDE : (h + 1) * WIDE] = sums[0]
    for h in range(HALVES):
        y_hop(h).wait_recv()
    agg = jnp.concatenate(
        [
            (keep[:, h * WIDE : (h + 1) * WIDE] + yr[h].astype(F32)).astype(BF16)
            for h in range(HALVES)
        ],
        axis=1,
    )

    preact = jnp.dot(agg, weight[...], preferred_element_type=F32)
    sigma = jax.nn.sigmoid(preact)
    active = preact * sigma
    out[...] = active.astype(BF16)
    label_line = jnp.broadcast_to(labels[pl.ds(team, 1), :], (128, 128))
    classes = lax.broadcasted_iota(jnp.int32, (128, 128), 0)
    onehot = (label_line == classes).astype(F32).T
    spare = jnp.zeros((120, 512), F32)
    wide_table = jnp.concatenate([table[...].astype(F32), spare], axis=0)
    target = jnp.dot(onehot, wide_table, preferred_element_type=F32)
    known = jnp.broadcast_to(mask[pl.ds(team, 1), :], (128, 128)).astype(F32).T
    known = jnp.concatenate([known] * 4, axis=1)
    residual = known * (active - target)
    slope = sigma * (1.0 + preact * (1.0 - sigma))
    grad_pre = (residual * slope).astype(BF16)
    back = lax.dot_general(
        grad_pre, weight[...], (((1,), (1,)), ((), ())), preferred_element_type=F32
    ).astype(BF16)
    gath[team] = back

    def cols(h):
        return pl.ds(h * WIDE, WIDE)

    def ag_hop(step, way, rel, h, device):
        sign = 1 if way == 0 else -1
        origin = block(z - sign * (step - 1), rel)
        ref = gath.at[origin, :, cols(h)]
        return remote(
            ref, ref, ag_send.at[way, step, rel, h], ag_recv.at[way, step, rel, h], device
        )

    def ag_wait(step, way, rel, h, device):
        sign = 1 if way == 0 else -1
        origin = block(z - sign * step, rel)
        ref = gath.at[origin, :, cols(h)]
        remote(
            ref, ref, ag_send.at[way, step, rel, h], ag_recv.at[way, step, rel, h], device
        ).wait_recv()

    def ag_side(h, slot):
        ref = gath.at[slot, :, cols(h)]
        return remote(ref, ref, y_send.at[2 + h], y_recv.at[2 + h], y_far)

    for h in range(HALVES):
        ag_side(h, team).start()
        for way, sign, device in ways:
            ag_hop(1, way, 0, h, device).start()
    gw = lax.dot_general(
        agg, grad_pre, (((0,), (0,)), ((), ())), preferred_element_type=F32
    ).reshape(16, 32, 512)
    gw32[...] = gw
    gwb[...] = gw.astype(BF16)

    def peer_row(d):
        return (rem(row + d, 16), team)

    def peer_team(d):
        return (row, rem(team + d, 16))

    def gw_hop(stage_id, d, receive):
        slot_row = rem(row - d + 16, 16) if receive else row
        slot_team = rem(team - d + 16, 16) if receive else team
        to_row, to_team = rem(row + d, 16), rem(team + d, 16)
        if stage_id == 0:
            src, dst, device = gwb.at[to_row], g1r.at[slot_row], peer_row(d)
        elif stage_id == 1:
            src, dst, device = g1t.at[to_team], g2r.at[slot_team], peer_team(d)
        elif stage_id == 2:
            src, dst, device = g3.at[slot_team], g3.at[slot_team], peer_team(d)
        else:
            src, dst, device = g4.at[slot_row], g4.at[slot_row], peer_row(d)
        return remote(
            src, dst, gw_send.at[stage_id, d], gw_recv.at[stage_id, d], device
        )

    def gw_start(stage_id):
        def one(d, carry):
            gw_hop(stage_id, d, False).start()
            return carry

        lax.fori_loop(1, 16, one, 0)

    def gw_arrive(stage_id):
        def one(d, carry):
            gw_hop(stage_id, d, True).wait_recv()
            return carry

        lax.fori_loop(1, 16, one, 0)

    def gw_stage(stage_id):
        gw_arrive(stage_id)
        if stage_id == 0:

            def one(d, total):
                return total + g1r[rem(row + d, 16)].astype(F32)

            total = lax.fori_loop(1, 16, one, gw32[row])
            for a in range(4):
                for b in range(4):
                    g1t[a * 4 + b] = total[a * 8 : a * 8 + 8, b * 128 : b * 128 + 128]
        elif stage_id == 1:

            def one(d, total):
                return total + g2r[rem(team + d, 16)]

            g3[team] = lax.fori_loop(1, 16, one, g1t[team])
        elif stage_id == 2:
            lines = [
                jnp.concatenate([g3[a * 4 + b] for b in range(4)], axis=1)
                for a in range(4)
            ]
            scale = 1.0 / math.sqrt(32768)
            g4[row] = (jnp.concatenate(lines, axis=0) * scale).astype(BF16)
        if stage_id < 3:
            gw_start(stage_id + 1)

    gw_start(0)
    for h in range(HALVES):
        ag_side(h, rem(team + 8, 16)).wait_recv()
        for way, sign, device in ways:
            ag_hop(1, way, 1, h, device).start()
    for step in range(2, 5):
        for rel in range(2):
            for h in range(HALVES):
                for way, sign, device in ways:
                    ag_wait(step - 1, way, rel, h, device)
                    if step < 4 or rel == way:
                        ag_hop(step, way, rel, h, device).start()
        gw_stage(step - 2)
    for rel in range(2):
        for h in range(HALVES):
            ag_wait(4, rel, rel, h, ways[rel][2])

    for k in range(16):
        product = jnp.dot(vt[k], gath[brow[k]], preferred_element_type=F32)
        slots[k] = product + slots[before(bcol, k)] if k else product
    for s in range(16):
        value = slots[final(bcol, s)].astype(BF16)
        for h in range(HALVES):
            sp[h, s % 2, s // 2] = value[:, h * WIDE : (h + 1) * WIDE]

    def p_hop(h):
        return remote(sp.at[h, 1 - core], prx.at[h], p_send.at[h], p_recv.at[h], partner)

    def chip_block(new_x, rel):
        return rem(ylo + rel, 2) * 4 + rem(new_x + 4, 4)

    x_ways = ((0, 1, x_up), (1, -1, x_down))

    def x_first(h, way, device):
        return remote(
            chip.at[h, chip_block(x + 2, way)],
            xr.at[way, 0, h, way],
            x_send.at[way, 0, h],
            x_recv.at[way, 0, h],
            device,
        )

    def x_hop(h, way, device):
        return remote(
            xs.at[way, h],
            xr.at[way, 1, h],
            x_send.at[way, 1, h],
            x_recv.at[way, 1, h],
            device,
        )

    def b_hop(h):
        return remote(bs.at[h], br.at[h], b_send.at[h], b_recv.at[h], y_side)

    for h in range(HALVES):
        p_hop(h).start()
    for h in range(HALVES):
        p_hop(h).wait_recv()

        def fold(m, carry, h=h):
            chip[h, m] = (sp[h, core, m].astype(F32) + prx[h, m].astype(F32)).astype(BF16)
            return carry

        lax.fori_loop(0, 8, fold, 0)
        for way, sign, device in x_ways:
            x_first(h, way, device).start()
    for h in range(HALVES):
        for way, sign, device in x_ways:
            x_first(h, way, device).wait_recv()
            for rel in range(2):
                value = chip[h, chip_block(x + sign, rel)]
                if rel == way:
                    value = (value.astype(F32) + xr[way, 0, h, rel].astype(F32)).astype(BF16)
                xs[way, h, rel] = value
            x_hop(h, way, device).start()
    for h in range(HALVES):
        for way, sign, device in x_ways:
            x_hop(h, way, device).wait_recv()
        sums = [
            chip[h, chip_block(x, rel)].astype(F32)
            + xr[0, 1, h, rel].astype(F32)
            + xr[1, 1, h, rel].astype(F32)
            for rel in range(2)
        ]
        bs[h] = sums[1].astype(BF16)
        b_hop(h).start()
        keep[:, h * WIDE : (h + 1) * WIDE] = sums[0]
    gw_stage(3)
    for a in range(16):
        gw_out[a * 32 : a * 32 + 32, :] = g4[a].astype(F32)
    for h in range(HALVES):
        b_hop(h).wait_recv()
        gf_out[:, h * WIDE : (h + 1) * WIDE] = (
            keep[:, h * WIDE : (h + 1) * WIDE] + br[h].astype(F32)
        ).astype(BF16)

    for h in range(HALVES):
        for way, sign, device in ways:
            z_first(h, way, sign, device).wait_send()
            for step in range(1, 4):
                z_hop(h, way, step, device).wait_send()
            for rel in range(2):
                for step in range(1, 5):
                    if step < 4 or rel == way:
                        ag_hop(step, way, rel, h, device).wait_send()
        y_hop(h).wait_send()
        ag_side(h, team).wait_send()
        p_hop(h).wait_send()
        b_hop(h).wait_send()
        for way, sign, device in x_ways:
            x_first(h, way, device).wait_send()
            x_hop(h, way, device).wait_send()

    def sent(d, carry):
        for stage_id in range(4):
            gw_hop(stage_id, d, False).wait_send()
        return carry

    lax.fori_loop(1, 16, sent, 0)


def per_device(
    features, weight, table, labels, label_mask, block_vals, block_row, block_col, block_count
):
    vmem = pl.BlockSpec(memory_space=pltpu.VMEM)
    smem = pl.BlockSpec(memory_space=pltpu.SMEM)
    dma = pltpu.SemaphoreType.DMA
    half = (HALVES, 128, WIDE)
    outs = pl.pallas_call(
        layer_kernel,
        out_shape=(
            jax.ShapeDtypeStruct((128, 512), BF16),
            jax.ShapeDtypeStruct((512, 512), F32),
            jax.ShapeDtypeStruct((128, 512), BF16),
        ),
        in_specs=[pl.BlockSpec(memory_space=pl.ANY)] + [vmem] * 5 + [smem] * 3,
        out_specs=(vmem, vmem, vmem),
        scratch_shapes=[
            pltpu.VMEM((16, 128, 512), BF16),
            pltpu.VMEM((16, 128, 128), BF16),
            pltpu.VMEM((17, 128, 512), F32),
            pltpu.VMEM((HALVES, 16, 128, WIDE), BF16),
            pltpu.VMEM((2, 4, HALVES, 2, 128, WIDE), BF16),
            pltpu.VMEM((2, 4, HALVES, 2, 128, WIDE), BF16),
            pltpu.VMEM(half, BF16),
            pltpu.VMEM(half, BF16),
            pltpu.VMEM((128, 512), F32),
            pltpu.VMEM((16, 128, 512), BF16),
            pltpu.VMEM((16, 32, 512), F32),
            pltpu.VMEM((16, 32, 512), BF16),
            pltpu.VMEM((16, 32, 512), BF16),
            pltpu.VMEM((16, 8, 128), F32),
            pltpu.VMEM((16, 8, 128), F32),
            pltpu.VMEM((16, 8, 128), F32),
            pltpu.VMEM((16, 32, 512), BF16),
            pltpu.VMEM((HALVES, 2, 8, 128, WIDE), BF16),
            pltpu.VMEM((HALVES, 8, 128, WIDE), BF16),
            pltpu.VMEM((HALVES, 8, 128, WIDE), BF16),
            pltpu.VMEM((2, HALVES, 2, 128, WIDE), BF16),
            pltpu.VMEM((2, 2, HALVES, 2, 128, WIDE), BF16),
            pltpu.VMEM(half, BF16),
            pltpu.VMEM(half, BF16),
            dma((32,)),
            dma((4, 32)),
            dma((2, 4, HALVES)),
            dma((2, 4, HALVES)),
            dma((4,)),
            dma((4,)),
            dma((2, 5, 2, HALVES)),
            dma((2, 5, 2, HALVES)),
            dma((4, 16)),
            dma((4, 16)),
            dma((HALVES,)),
            dma((HALVES,)),
            dma((2, 2, HALVES)),
            dma((2, 2, HALVES)),
            dma((HALVES,)),
            dma((HALVES,)),
        ],
        compiler_params=pltpu.CompilerParams(collective_id=0, has_side_effects=True),
        name="layer",
    )(
        features,
        weight,
        table,
        labels.reshape(16, 128),
        label_mask.reshape(16, 128),
        block_vals[0, 0],
        block_row[0, 0],
        block_col[0, 0],
        block_count[0],
    )
    output, grad_weight, grad_piece = outs
    return (output, grad_weight, grad_piece[None])


def solution(mesh):
    placed = (
        P("row", None),
        P(),
        P(),
        P("row"),
        P("row"),
        P("row", "team", None, None, None),
        P("row", "team", None),
        P("row", "team", None),
        P("row", "team"),
    )
    return jax.shard_map(
        per_device,
        mesh=mesh,
        in_specs=placed,
        out_specs=(P(("row", "team"), None), P(), P("team", "row", None)),
        check_vma=False,
    )
```

time: 611 us -> 146 us (0.24)
  waiting for transfers between devices: 435 us -> 0 us
  Pallas kernels: 0 us -> 140 us
  blocking collectives: 98.9 us -> 0 us
  local copies, waits for them, and re-layouts: 31.2 us -> 4.52 us
  matrix products: 19.5 us -> 0 us
  between operations: 14.6 us -> 1.3 us
  other arithmetic: 8.34 us -> 0 us
    psum x2 -> x0, waiting for transfers between devices: 368 us -> none  [the longest x1 236 us: per_device(): lax.psum(weight_term, ('row', 'team'))]
    pallas_call x0 -> x1, Pallas kernels: none -> 140 us  [per_device(): pl.pallas_call(layer_kernel, out_shape=(jax.ShapeDtypeStruct((128, 512),...]
    psum x1 -> x0, blocking collectives: 98.9 us -> none  [per_device(): summed = lax.psum(partial_value, 'team')]
    reduce_scatter x1 -> x0, waiting for transfers between devices: 67.3 us -> none  [per_device(): lax.psum_scatter(spread, 'row', scatter_dimension=0, tiled=True)]
    dot_general x10 -> x0, matrix products: 19.5 us -> none  [the longest x2 4.78 us: add_group(): jnp.einsum('sk,kif->sif', selector, lower, preferred_element_type=jnp.flo...]
    while x10 -> x0, local copies, waits for them, and re-layouts: 18.8 us -> none  [the longest x2 13.2 us: block_product(): lax.fori_loop(jnp.int32(0), groups, add_group, jnp.zeros((out_blocks, 128...]
  transfers between devices with their start and end apart: 3 -> 0, of which waited for: 3 -> 0; matrix products, arithmetic and copies ran while one was open for 4% -> 0% of each run, Pallas kernels for 0% -> 0%
where the time goes in v1:
time: 146 us
  Pallas kernels  140 us (96%)
  local copies, waits for them, and re-layouts  4.52 us (3%)
    pallas_call x1, Pallas kernels, per_device(): pl.pallas_call(layer_kernel, out_shape=(jax.ShapeDtypeStruct((128, 512),...  140 us
    unnamed x5, local copies, waits for them, and re-layouts  4.52 us

profile of v1, /device:TPU:1, one launch (start us, length us, event | category | flops | bytes accessed | tf_op | source)
XLA Modules:
  0.0 146.2 jit_solution(16785507676300717634)
XLA Ops:
  1.3 140.4 %layer.1 = (bf16[128,512]{1,0:T(8,128)(2,1)}, f32[512,512]{1,0:T(8,128)}, bf16[128,512]{1,0:T(8,128)(2,1)}) custom-call(bf16[2048,512]{1,0:T(8,128)(2,1)} %feat.1, bf16[512,512]{1,0:T(8,128)(2,1)} %weight.1, bf16[8,512]{1,0:T(8,128)(2,1)} %table.1, s32[16,128]{1,0:T(8,128)} %bitcast.10, s32[16,128]{1,0:T(8,128)} %bitcast.11, bf16[16,128,128]{2,1,0:T(8,128)(2,1)} %bitcast.8, ...), custom_call_target="tpu_custom_call" | custom-call | tf_op jit(solution)/shard_map/layer/pallas_call | solution.py:589
  141.7 0.0 copy-start
  141.7 1.6 %copy.16 = bf16[128,512]{1,0:T(8,128)(2,1)} copy(bf16[128,512]{1,0:T(8,128)(2,1)} %get-tuple-element.12) | data formatting | bytes 262144
  143.3 2.3 %copy.17 = f32[512,512]{1,0:T(8,128)} copy(f32[512,512]{1,0:T(8,128)} %get-tuple-element.13) | data formatting | bytes 2097152
  145.6 0.0 copy-done
  145.6 0.7 copy.18
Async XLA Ops:
  141.7 3.9 %copy-start = (bf16[128,512]{1,0:T(8,128)(2,1)S(1)}, bf16[128,512]{1,0:T(8,128)(2,1)}, u32[]{:S(2)}) copy-start(bf16[128,512]{1,0:T(8,128)(2,1)} %get-tuple-element.8) | copy-start | bytes 393220

commit v2 on v1

--- a/solution.py
+++ b/solution.py
@@ -11,11 +11,15 @@
 MESH = pl.DeviceIdType.MESH
 BF16 = jnp.bfloat16
 F32 = jnp.float32
-HALVES = 2
-WIDE = 256
-PIECE = 64
-TREES = ((0, 11), (11, 10), (21, 11))
+PARTS = 4
+WIDE = 128
+AG_PARTS = 2
+AG_WIDE = 256
+PIECE = 32
+TREES = ((0, 22), (22, 20), (42, 22))
+LONGEST = 22
 DEEPEST = 5
+LAG = 9
 
 
 def rem(value, size):
@@ -140,7 +144,10 @@
     pieces = feat.shape[0] // PIECE
 
     def landed(piece):
-        return xv.at[div(piece, 2), pl.ds(pl.multiple_of(rem(piece, 2) * PIECE, PIECE), PIECE)]
+        return xv.at[
+            div(piece, 128 // PIECE),
+            pl.ds(pl.multiple_of(rem(piece, 128 // PIECE) * PIECE, PIECE), PIECE),
+        ]
 
     def stage(piece):
         return pltpu.make_async_copy(
@@ -201,7 +208,7 @@
     def _():
         def beat(tick, carry):
             for tree, (first, number) in enumerate(TREES):
-                q = tick - depths[tree]
+                q = tick - LAG * depths[tree]
 
                 @pl.when((q >= 0) & (q < number))
                 def _(tree=tree, first=first, q=q):
@@ -225,7 +232,7 @@
 
             return carry
 
-        lax.fori_loop(0, 11 + DEEPEST, beat, 0)
+        lax.fori_loop(0, LONGEST + LAG * DEEPEST, beat, 0)
 
         def settle(q, carry):
             for tree, (first, number) in enumerate(TREES):
@@ -242,7 +249,7 @@
 
             return carry
 
-        lax.fori_loop(0, 11, settle, 0)
+        lax.fori_loop(0, LONGEST, settle, 0)
 
     @pl.when(jnp.logical_not(lead))
     def _():
@@ -272,7 +279,7 @@
         slots[k] = product + slots[before(brow, k)] if k else product
     for s in range(16):
         value = slots[final(brow, s)].astype(BF16)
-        for h in range(HALVES):
+        for h in range(PARTS):
             part[h, s] = value[:, h * WIDE : (h + 1) * WIDE]
 
     def block(new_z, rel):
@@ -298,11 +305,11 @@
             device,
         )
 
-    for h in range(HALVES):
+    for h in range(PARTS):
         for way, sign, device in ways:
             z_first(h, way, sign, device).start()
     for step in range(1, 4):
-        for h in range(HALVES):
+        for h in range(PARTS):
             for way, sign, device in ways:
                 if step == 1:
                     z_first(h, way, sign, device).wait_recv()
@@ -320,7 +327,7 @@
     def y_hop(h):
         return remote(ys.at[h], yr.at[h], y_send.at[h], y_recv.at[h], y_far)
 
-    for h in range(HALVES):
+    for h in range(PARTS):
         for way, sign, device in ways:
             z_hop(h, way, 3, device).wait_recv()
         sums = [
@@ -332,12 +339,12 @@
         ys[h] = sums[1].astype(BF16)
         y_hop(h).start()
         keep[:, h * WIDE : (h + 1) * WIDE] = sums[0]
-    for h in range(HALVES):
+    for h in range(PARTS):
         y_hop(h).wait_recv()
     agg = jnp.concatenate(
         [
             (keep[:, h * WIDE : (h + 1) * WIDE] + yr[h].astype(F32)).astype(BF16)
-            for h in range(HALVES)
+            for h in range(PARTS)
         ],
         axis=1,
     )
@@ -363,7 +370,7 @@
     gath[team] = back
 
     def cols(h):
-        return pl.ds(h * WIDE, WIDE)
+        return pl.ds(h * AG_WIDE, AG_WIDE)
 
     def ag_hop(step, way, rel, h, device):
         sign = 1 if way == 0 else -1
@@ -383,9 +390,9 @@
 
     def ag_side(h, slot):
         ref = gath.at[slot, :, cols(h)]
-        return remote(ref, ref, y_send.at[2 + h], y_recv.at[2 + h], y_far)
-
-    for h in range(HALVES):
+        return remote(ref, ref, y_send.at[PARTS + h], y_recv.at[PARTS + h], y_far)
+
+    for h in range(AG_PARTS):
         ag_side(h, team).start()
         for way, sign, device in ways:
             ag_hop(1, way, 0, h, device).start()
@@ -459,20 +466,20 @@
             gw_start(stage_id + 1)
 
     gw_start(0)
-    for h in range(HALVES):
+    for h in range(AG_PARTS):
         ag_side(h, rem(team + 8, 16)).wait_recv()
         for way, sign, device in ways:
             ag_hop(1, way, 1, h, device).start()
     for step in range(2, 5):
         for rel in range(2):
-            for h in range(HALVES):
+            for h in range(AG_PARTS):
                 for way, sign, device in ways:
                     ag_wait(step - 1, way, rel, h, device)
                     if step < 4 or rel == way:
                         ag_hop(step, way, rel, h, device).start()
         gw_stage(step - 2)
     for rel in range(2):
-        for h in range(HALVES):
+        for h in range(AG_PARTS):
             ag_wait(4, rel, rel, h, ways[rel][2])
 
     for k in range(16):
@@ -480,7 +487,7 @@
         slots[k] = product + slots[before(bcol, k)] if k else product
     for s in range(16):
         value = slots[final(bcol, s)].astype(BF16)
-        for h in range(HALVES):
+        for h in range(PARTS):
             sp[h, s % 2, s // 2] = value[:, h * WIDE : (h + 1) * WIDE]
 
     def p_hop(h):
@@ -512,9 +519,9 @@
     def b_hop(h):
         return remote(bs.at[h], br.at[h], b_send.at[h], b_recv.at[h], y_side)
 
-    for h in range(HALVES):
+    for h in range(PARTS):
         p_hop(h).start()
-    for h in range(HALVES):
+    for h in range(PARTS):
         p_hop(h).wait_recv()
 
         def fold(m, carry, h=h):
@@ -524,7 +531,7 @@
         lax.fori_loop(0, 8, fold, 0)
         for way, sign, device in x_ways:
             x_first(h, way, device).start()
-    for h in range(HALVES):
+    for h in range(PARTS):
         for way, sign, device in x_ways:
             x_first(h, way, device).wait_recv()
             for rel in range(2):
@@ -533,7 +540,7 @@
                     value = (value.astype(F32) + xr[way, 0, h, rel].astype(F32)).astype(BF16)
                 xs[way, h, rel] = value
             x_hop(h, way, device).start()
-    for h in range(HALVES):
+    for h in range(PARTS):
         for way, sign, device in x_ways:
             x_hop(h, way, device).wait_recv()
         sums = [
@@ -546,30 +553,31 @@
         b_hop(h).start()
         keep[:, h * WIDE : (h + 1) * WIDE] = sums[0]
     gw_stage(3)
-    for a in range(16):
-        gw_out[a * 32 : a * 32 + 32, :] = g4[a].astype(F32)
-    for h in range(HALVES):
+    gw_out[...] = g4[...]
+    for h in range(PARTS):
         b_hop(h).wait_recv()
         gf_out[:, h * WIDE : (h + 1) * WIDE] = (
             keep[:, h * WIDE : (h + 1) * WIDE] + br[h].astype(F32)
         ).astype(BF16)
 
-    for h in range(HALVES):
+    for h in range(PARTS):
         for way, sign, device in ways:
             z_first(h, way, sign, device).wait_send()
             for step in range(1, 4):
                 z_hop(h, way, step, device).wait_send()
-            for rel in range(2):
-                for step in range(1, 5):
-                    if step < 4 or rel == way:
-                        ag_hop(step, way, rel, h, device).wait_send()
         y_hop(h).wait_send()
-        ag_side(h, team).wait_send()
         p_hop(h).wait_send()
         b_hop(h).wait_send()
         for way, sign, device in x_ways:
             x_first(h, way, device).wait_send()
             x_hop(h, way, device).wait_send()
+    for h in range(AG_PARTS):
+        ag_side(h, team).wait_send()
+        for way, sign, device in ways:
+            for rel in range(2):
+                for step in range(1, 5):
+                    if step < 4 or rel == way:
+                        ag_hop(step, way, rel, h, device).wait_send()
 
     def sent(d, carry):
         for stage_id in range(4):
@@ -585,12 +593,12 @@
     vmem = pl.BlockSpec(memory_space=pltpu.VMEM)
     smem = pl.BlockSpec(memory_space=pltpu.SMEM)
     dma = pltpu.SemaphoreType.DMA
-    half = (HALVES, 128, WIDE)
+    half = (PARTS, 128, WIDE)
     outs = pl.pallas_call(
         layer_kernel,
         out_shape=(
             jax.ShapeDtypeStruct((128, 512), BF16),
-            jax.ShapeDtypeStruct((512, 512), F32),
+            jax.ShapeDtypeStruct((16, 32, 512), BF16),
             jax.ShapeDtypeStruct((128, 512), BF16),
         ),
         in_specs=[pl.BlockSpec(memory_space=pl.ANY)] + [vmem] * 5 + [smem] * 3,
@@ -599,9 +607,9 @@
             pltpu.VMEM((16, 128, 512), BF16),
             pltpu.VMEM((16, 128, 128), BF16),
             pltpu.VMEM((17, 128, 512), F32),
-            pltpu.VMEM((HALVES, 16, 128, WIDE), BF16),
-            pltpu.VMEM((2, 4, HALVES, 2, 128, WIDE), BF16),
-            pltpu.VMEM((2, 4, HALVES, 2, 128, WIDE), BF16),
+            pltpu.VMEM((PARTS, 16, 128, WIDE), BF16),
+            pltpu.VMEM((2, 4, PARTS, 2, 128, WIDE), BF16),
+            pltpu.VMEM((2, 4, PARTS, 2, 128, WIDE), BF16),
             pltpu.VMEM(half, BF16),
             pltpu.VMEM(half, BF16),
             pltpu.VMEM((128, 512), F32),
@@ -613,29 +621,29 @@
             pltpu.VMEM((16, 8, 128), F32),
             pltpu.VMEM((16, 8, 128), F32),
             pltpu.VMEM((16, 32, 512), BF16),
-            pltpu.VMEM((HALVES, 2, 8, 128, WIDE), BF16),
-            pltpu.VMEM((HALVES, 8, 128, WIDE), BF16),
-            pltpu.VMEM((HALVES, 8, 128, WIDE), BF16),
-            pltpu.VMEM((2, HALVES, 2, 128, WIDE), BF16),
-            pltpu.VMEM((2, 2, HALVES, 2, 128, WIDE), BF16),
+            pltpu.VMEM((PARTS, 2, 8, 128, WIDE), BF16),
+            pltpu.VMEM((PARTS, 8, 128, WIDE), BF16),
+            pltpu.VMEM((PARTS, 8, 128, WIDE), BF16),
+            pltpu.VMEM((2, PARTS, 2, 128, WIDE), BF16),
+            pltpu.VMEM((2, 2, PARTS, 2, 128, WIDE), BF16),
             pltpu.VMEM(half, BF16),
             pltpu.VMEM(half, BF16),
-            dma((32,)),
-            dma((4, 32)),
-            dma((2, 4, HALVES)),
-            dma((2, 4, HALVES)),
-            dma((4,)),
-            dma((4,)),
-            dma((2, 5, 2, HALVES)),
-            dma((2, 5, 2, HALVES)),
+            dma((64,)),
+            dma((4, 64)),
+            dma((2, 4, PARTS)),
+            dma((2, 4, PARTS)),
+            dma((PARTS + AG_PARTS,)),
+            dma((PARTS + AG_PARTS,)),
+            dma((2, 5, 2, AG_PARTS)),
+            dma((2, 5, 2, AG_PARTS)),
             dma((4, 16)),
             dma((4, 16)),
-            dma((HALVES,)),
-            dma((HALVES,)),
-            dma((2, 2, HALVES)),
-            dma((2, 2, HALVES)),
-            dma((HALVES,)),
-            dma((HALVES,)),
+            dma((PARTS,)),
+            dma((PARTS,)),
+            dma((2, 2, PARTS)),
+            dma((2, 2, PARTS)),
+            dma((PARTS,)),
+            dma((PARTS,)),
         ],
         compiler_params=pltpu.CompilerParams(collective_id=0, has_side_effects=True),
         name="layer",
@@ -651,7 +659,7 @@
         block_count[0],
     )
     output, grad_weight, grad_piece = outs
-    return (output, grad_weight, grad_piece[None])
+    return (output, grad_weight.reshape(512, 512).astype(F32), grad_piece[None])
 
 
 def solution(mesh):

time: 146 us -> 123 us (0.84)
  Pallas kernels: 140 us -> 117 us
  other arithmetic: 0 us -> 2.15 us
    pallas_call x1, Pallas kernels: 140 us -> 117 us  [per_device(): pl.pallas_call(layer_kernel, out_shape=(jax.ShapeDtypeStruct((128, 512),...]
    convert_element_type x0 -> x1, other arithmetic: none -> 2.15 us  [per_device(): return (output, grad_weight.reshape(512, 512).astype(F32), grad_piece[None])]
    unnamed x5 -> x2, local copies, waits for them, and re-layouts: 4.52 us -> 3.13 us
where the time goes in v2:
time: 123 us
  Pallas kernels  117 us (95%)
  local copies, waits for them, and re-layouts  3.13 us (3%)
  other arithmetic  2.15 us (2%)
  between operations  1.29 us (1%)
    pallas_call x1, Pallas kernels, per_device(): pl.pallas_call(layer_kernel, out_shape=(jax.ShapeDtypeStruct((128, 512),...  117 us
    unnamed x2, local copies, waits for them, and re-layouts  3.13 us

profile of v2, /device:TPU:1, one launch (start us, length us, event | category | flops | bytes accessed | tf_op | source)
XLA Modules:
  0.0 123.2 jit_solution(13118353213831293743)
XLA Ops:
  1.3 116.6 %layer.1 = (bf16[128,512]{1,0:T(8,128)(2,1)}, bf16[16,32,512]{2,1,0:T(8,128)(2,1)}, bf16[128,512]{1,0:T(8,128)(2,1)}) custom-call(bf16[2048,512]{1,0:T(8,128)(2,1)} %feat.1, bf16[512,512]{1,0:T(8,128)(2,1)} %weight.1, bf16[8,512]{1,0:T(8,128)(2,1)} %table.1, s32[16,128]{1,0:T(8,128)} %bitcast.13, s32[16,128]{1,0:T(8,128)} %bitcast.14, ...), custom_call_target="tpu_custom_call" | custom-call | tf_op jit(solution)/shard_map/layer/pallas_call | solution.py:597
  117.9 2.1 %bitcast_convert_fusion = f32[512,512]{1,0:T(8,128)} fusion(bf16[16,32,512]{2,1,0:T(8,128)(2,1)} %get-tuple-element.7), kind=kLoop, calls=%fused_computation | loop fusion | flops 262144 | bytes 1572864 | tf_op jit(solution)/shard_map/convert_element_type | solution.py:662
  120.0 1.6 %copy.15 = bf16[128,512]{1,0:T(8,128)(2,1)} copy(bf16[128,512]{1,0:T(8,128)(2,1)} %get-tuple-element.12) | data formatting | bytes 262144
  121.6 1.6 %copy.16 = bf16[1,128,512]{2,1,0:T(8,128)(2,1)} copy(bf16[1,128,512]{2,1,0:T(8,128)(2,1)} %bitcast.12) | data formatting | bytes 262144

commit v3 on v2

--- a/solution.py
+++ b/solution.py
@@ -18,7 +18,8 @@
 PIECE = 32
 TREES = ((0, 22), (22, 20), (42, 22))
 LONGEST = 22
-DEEPEST = 5
+DEEPEST = 4
+FED = 42
 LAG = 9
 
 
@@ -87,6 +88,7 @@
     br,
     bc_recv,
     bc_send,
+    feed_send,
     z_send,
     z_recv,
     y_send,
@@ -134,6 +136,8 @@
         return carry
 
     lax.fori_loop(1, 16, greet, 0)
+    fed = (((1 - ylo) * 4 + x) * 2 + core, rem(team + 8, 16))
+    pl.semaphore_signal(barrier, inc=1, device_id=fed, device_id_type=MESH)
 
     root = team
     root_core = rem(root, 2)
@@ -168,22 +172,46 @@
     for k in range(16):
         vt[k] = vals[k].T
 
-    pl.semaphore_wait(barrier, 30)
+    pl.semaphore_wait(barrier, 31)
+
+    feeder = row == rem(team + 8, 16)
+
+    def feed(piece):
+        return remote(
+            feat.at[pl.ds(pl.multiple_of(piece * PIECE, PIECE), PIECE)],
+            landed(piece),
+            feed_send.at[piece],
+            bc_recv.at[piece],
+            fed,
+        )
+
+    @pl.when(feeder)
+    def _():
+        def begin(q, carry):
+            feed(q).start()
+
+            @pl.when(q < TREES[1][1])
+            def _():
+                feed(TREES[1][0] + q).start()
+
+            return carry
+
+        lax.fori_loop(0, LONGEST, begin, 0)
 
     low = ry == 0
     depths = (
-        jnp.where(low, pick(rx, (0, 1, 2, 3)), pick(rx, (5, 2, 3, 4))),
-        jnp.where(low, pick(rx, (0, 3, 2, 1)), pick(rx, (5, 4, 3, 2))),
+        jnp.where(low, pick(rx, (0, 1, 2, 3)), pick(rx, (3, 2, 3, 4))),
+        jnp.where(low, pick(rx, (0, 3, 2, 1)), pick(rx, (3, 4, 3, 2))),
         jnp.where(low, pick(rx, (0, 3, 4, 3)), pick(rx, (1, 2, 3, 2))),
     )
     ups = (
-        (low & (rx < 3)) | (~low & (rx > 1)),
+        (low & (rx < 3)) | (~low & (rx == 2)),
         None,
         ~low & (rx < 2),
     )
     downs = (
         None,
-        (low & (rx != 1)) | (~low & (rx > 0)),
+        (low & (rx != 1)) | (~low & (rx > 1)),
         ~low & (rx == 0),
     )
     sides = (
@@ -233,23 +261,6 @@
             return carry
 
         lax.fori_loop(0, LONGEST + LAG * DEEPEST, beat, 0)
-
-        def settle(q, carry):
-            for tree, (first, number) in enumerate(TREES):
-
-                @pl.when(q < number)
-                def _(tree=tree, first=first):
-                    for way, condition, device in branches(tree):
-                        if condition is None:
-                            continue
-
-                        @pl.when(condition)
-                        def _(way=way, device=device):
-                            hop(first + q, way, device).wait_send()
-
-            return carry
-
-        lax.fori_loop(0, LONGEST, settle, 0)
 
     @pl.when(jnp.logical_not(lead))
     def _():
@@ -308,6 +319,34 @@
     for h in range(PARTS):
         for way, sign, device in ways:
             z_first(h, way, sign, device).start()
+
+    @pl.when(lead)
+    def _():
+        def settle(q, carry):
+            for tree, (first, number) in enumerate(TREES):
+
+                @pl.when(q < number)
+                def _(tree=tree, first=first):
+                    for way, condition, device in branches(tree):
+                        if condition is None:
+                            continue
+
+                        @pl.when(condition)
+                        def _(way=way, device=device):
+                            hop(first + q, way, device).wait_send()
+
+            return carry
+
+        lax.fori_loop(0, LONGEST, settle, 0)
+
+    @pl.when(feeder)
+    def _():
+        def fed_all(piece, carry):
+            feed(piece).wait_send()
+            return carry
+
+        lax.fori_loop(0, FED, fed_all, 0)
+
     for step in range(1, 4):
         for h in range(PARTS):
             for way, sign, device in ways:
@@ -419,7 +458,8 @@
         elif stage_id == 2:
             src, dst, device = g3.at[slot_team], g3.at[slot_team], peer_team(d)
         else:
-            src, dst, device = g4.at[slot_row], g4.at[slot_row], peer_row(d)
+            spot = g4.at[div(slot_row, 2), rem(slot_row, 2)]
+            src, dst, device = spot, spot, peer_row(d)
         return remote(
             src, dst, gw_send.at[stage_id, d], gw_recv.at[stage_id, d], device
         )
@@ -461,11 +501,24 @@
                 for a in range(4)
             ]
             scale = 1.0 / math.sqrt(32768)
-            g4[row] = (jnp.concatenate(lines, axis=0) * scale).astype(BF16)
-        if stage_id < 3:
+            g4[div(row, 2), core] = (jnp.concatenate(lines, axis=0) * scale).astype(BF16)
+        if stage_id < 2:
             gw_start(stage_id + 1)
+        else:
+            for d in range(2, 16, 2):
+                gw_hop(3, d, False).start()
+
+    def gw_across(receive):
+        side = g4.at[:, 1 - core if receive else core]
+        return remote(side, side, gw_send.at[3, 1], gw_recv.at[3, 1], partner)
 
     gw_start(0)
+    for h in range(PARTS):
+        for way, sign, device in ways:
+            z_first(h, way, sign, device).wait_send()
+            for step in range(1, 4):
+                z_hop(h, way, step, device).wait_send()
+        y_hop(h).wait_send()
     for h in range(AG_PARTS):
         ag_side(h, rem(team + 8, 16)).wait_recv()
         for way, sign, device in ways:
@@ -477,10 +530,12 @@
                     ag_wait(step - 1, way, rel, h, device)
                     if step < 4 or rel == way:
                         ag_hop(step, way, rel, h, device).start()
-        gw_stage(step - 2)
+        if step == 3:
+            gw_stage(0)
     for rel in range(2):
         for h in range(AG_PARTS):
             ag_wait(4, rel, rel, h, ways[rel][2])
+    gw_stage(1)
 
     for k in range(16):
         product = jnp.dot(vt[k], gath[brow[k]], preferred_element_type=F32)
@@ -521,6 +576,7 @@
 
     for h in range(PARTS):
         p_hop(h).start()
+    gw_stage(2)
     for h in range(PARTS):
         p_hop(h).wait_recv()
 
@@ -531,6 +587,20 @@
         lax.fori_loop(0, 8, fold, 0)
         for way, sign, device in x_ways:
             x_first(h, way, device).start()
+    for h in range(AG_PARTS):
+        ag_side(h, team).wait_send()
+        for way, sign, device in ways:
+            for rel in range(2):
+                for step in range(1, 5):
+                    if step < 4 or rel == way:
+                        ag_hop(step, way, rel, h, device).wait_send()
+
+    def sent(d, carry):
+        for stage_id in range(3):
+            gw_hop(stage_id, d, False).wait_send()
+        return carry
+
+    lax.fori_loop(1, 16, sent, 0)
     for h in range(PARTS):
         for way, sign, device in x_ways:
             x_first(h, way, device).wait_recv()
@@ -552,39 +622,26 @@
         bs[h] = sums[1].astype(BF16)
         b_hop(h).start()
         keep[:, h * WIDE : (h + 1) * WIDE] = sums[0]
-    gw_stage(3)
-    gw_out[...] = g4[...]
+    for d in range(2, 16, 2):
+        gw_hop(3, d, True).wait_recv()
+    gw_across(False).start()
     for h in range(PARTS):
         b_hop(h).wait_recv()
         gf_out[:, h * WIDE : (h + 1) * WIDE] = (
             keep[:, h * WIDE : (h + 1) * WIDE] + br[h].astype(F32)
         ).astype(BF16)
 
-    for h in range(PARTS):
-        for way, sign, device in ways:
-            z_first(h, way, sign, device).wait_send()
-            for step in range(1, 4):
-                z_hop(h, way, step, device).wait_send()
-        y_hop(h).wait_send()
+    gw_across(True).wait_recv()
+    gw_out[...] = g4[...].reshape(16, 32, 512)
+    for d in range(2, 16, 2):
+        gw_hop(3, d, False).wait_send()
+    gw_across(False).wait_send()
+    for h in range(PARTS):
         p_hop(h).wait_send()
         b_hop(h).wait_send()
         for way, sign, device in x_ways:
             x_first(h, way, device).wait_send()
             x_hop(h, way, device).wait_send()
-    for h in range(AG_PARTS):
-        ag_side(h, team).wait_send()
-        for way, sign, device in ways:
-            for rel in range(2):
-                for step in range(1, 5):
-                    if step < 4 or rel == way:
-                        ag_hop(step, way, rel, h, device).wait_send()
-
-    def sent(d, carry):
-        for stage_id in range(4):
-            gw_hop(stage_id, d, False).wait_send()
-        return carry
-
-    lax.fori_loop(1, 16, sent, 0)
 
 
 def per_device(
@@ -620,7 +677,7 @@
             pltpu.VMEM((16, 8, 128), F32),
             pltpu.VMEM((16, 8, 128), F32),
             pltpu.VMEM((16, 8, 128), F32),
-            pltpu.VMEM((16, 32, 512), BF16),
+            pltpu.VMEM((8, 2, 32, 512), BF16),
             pltpu.VMEM((PARTS, 2, 8, 128, WIDE), BF16),
             pltpu.VMEM((PARTS, 8, 128, WIDE), BF16),
             pltpu.VMEM((PARTS, 8, 128, WIDE), BF16),
@@ -630,6 +687,7 @@
             pltpu.VMEM(half, BF16),
             dma((64,)),
             dma((4, 64)),
+            dma((64,)),
             dma((2, 4, PARTS)),
             dma((2, 4, PARTS)),
             dma((PARTS + AG_PARTS,)),

time: 123 us -> 123 us (level)
  no operation moved by 1% of the time
where the time goes in v3:
time: 123 us; the launch traced here: 122 us
  Pallas kernels  116 us (94%)
  local copies, waits for them, and re-layouts  3.13 us (3%)
  other arithmetic  2.15 us (2%)
  between operations  1.29 us (1%)
    pallas_call x1, Pallas kernels, per_device(): pl.pallas_call(layer_kernel, out_shape=(jax.ShapeDtypeStruct((128, 512),...  116 us
    unnamed x2, local copies, waits for them, and re-layouts  3.13 us

profile of v3, /device:TPU:1, one launch (start us, length us, event | category | flops | bytes accessed | tf_op | source)
XLA Modules:
  0.0 122.1 jit_solution(3690980615351738868)
XLA Ops:
  1.3 115.5 %layer.1 = (bf16[128,512]{1,0:T(8,128)(2,1)}, bf16[16,32,512]{2,1,0:T(8,128)(2,1)}, bf16[128,512]{1,0:T(8,128)(2,1)}) custom-call(bf16[2048,512]{1,0:T(8,128)(2,1)} %feat.1, bf16[512,512]{1,0:T(8,128)(2,1)} %weight.1, bf16[8,512]{1,0:T(8,128)(2,1)} %table.1, s32[16,128]{1,0:T(8,128)} %bitcast.13, s32[16,128]{1,0:T(8,128)} %bitcast.14, ...), custom_call_target="tpu_custom_call" | custom-call | tf_op jit(solution)/shard_map/layer/pallas_call | solution.py:654
  116.8 2.1 %bitcast_convert_fusion = f32[512,512]{1,0:T(8,128)} fusion(bf16[16,32,512]{2,1,0:T(8,128)(2,1)} %get-tuple-element.7), kind=kLoop, calls=%fused_computation | loop fusion | flops 262144 | bytes 1572864 | tf_op jit(solution)/shard_map/convert_element_type | solution.py:720
  118.9 1.6 %copy.15 = bf16[128,512]{1,0:T(8,128)(2,1)} copy(bf16[128,512]{1,0:T(8,128)(2,1)} %get-tuple-element.12) | data formatting | bytes 262144
  120.5 1.6 %copy.16 = bf16[1,128,512]{2,1,0:T(8,128)(2,1)} copy(bf16[1,128,512]{2,1,0:T(8,128)(2,1)} %bitcast.12) | data formatting | bytes 262144

commit v4 on v3

--- a/solution.py
+++ b/solution.py
@@ -74,6 +74,9 @@
     gath,
     gw32,
     gwb,
+    gcr,
+    gc32,
+    gcb,
     g1r,
     g1t,
     g2r,
@@ -431,15 +434,21 @@
         ref = gath.at[slot, :, cols(h)]
         return remote(ref, ref, y_send.at[PARTS + h], y_recv.at[PARTS + h], y_far)
 
+    def gw_pair():
+        return remote(
+            gwb.at[:, 1 - core], gcr, gw_send.at[0, 1], gw_recv.at[0, 1], partner
+        )
+
     for h in range(AG_PARTS):
         ag_side(h, team).start()
         for way, sign, device in ways:
             ag_hop(1, way, 0, h, device).start()
     gw = lax.dot_general(
         agg, grad_pre, (((0,), (0,)), ((), ())), preferred_element_type=F32
-    ).reshape(16, 32, 512)
+    ).reshape(8, 2, 32, 512)
     gw32[...] = gw
     gwb[...] = gw.astype(BF16)
+    gw_pair().start()
 
     def peer_row(d):
         return (rem(row + d, 16), team)
@@ -452,7 +461,7 @@
         slot_team = rem(team - d + 16, 16) if receive else team
         to_row, to_team = rem(row + d, 16), rem(team + d, 16)
         if stage_id == 0:
-            src, dst, device = gwb.at[to_row], g1r.at[slot_row], peer_row(d)
+            src, dst, device = gcb.at[div(to_row, 2)], g1r.at[div(slot_row, 2)], peer_row(d)
         elif stage_id == 1:
             src, dst, device = g1t.at[to_team], g2r.at[slot_team], peer_team(d)
         elif stage_id == 2:
@@ -464,37 +473,41 @@
             src, dst, gw_send.at[stage_id, d], gw_recv.at[stage_id, d], device
         )
 
+    def peers(stage_id):
+        return range(2, 16, 2) if stage_id in (0, 3) else range(1, 16)
+
     def gw_start(stage_id):
-        def one(d, carry):
+        for d in peers(stage_id):
             gw_hop(stage_id, d, False).start()
-            return carry
-
-        lax.fori_loop(1, 16, one, 0)
 
     def gw_arrive(stage_id):
-        def one(d, carry):
+        for d in peers(stage_id):
             gw_hop(stage_id, d, True).wait_recv()
-            return carry
-
-        lax.fori_loop(1, 16, one, 0)
+
+    def gw_chip():
+        gw_pair().wait_recv()
+        for m in range(8):
+            both = gw32[m, core] + gcr[m].astype(F32)
+            gc32[m] = both
+            gcb[m] = both.astype(BF16)
+        gw_start(0)
 
     def gw_stage(stage_id):
         gw_arrive(stage_id)
         if stage_id == 0:
 
-            def one(d, total):
-                return total + g1r[rem(row + d, 16)].astype(F32)
-
-            total = lax.fori_loop(1, 16, one, gw32[row])
+            total = gc32[div(row, 2)]
+            for d in range(1, 8):
+                total = total + g1r[rem(div(row, 2) + d, 8)].astype(F32)
             for a in range(4):
                 for b in range(4):
                     g1t[a * 4 + b] = total[a * 8 : a * 8 + 8, b * 128 : b * 128 + 128]
         elif stage_id == 1:
 
-            def one(d, total):
-                return total + g2r[rem(team + d, 16)]
-
-            g3[team] = lax.fori_loop(1, 16, one, g1t[team])
+            total = g1t[team]
+            for d in range(1, 16):
+                total = total + g2r[rem(team + d, 16)]
+            g3[team] = total
         elif stage_id == 2:
             lines = [
                 jnp.concatenate([g3[a * 4 + b] for b in range(4)], axis=1)
@@ -502,35 +515,34 @@
             ]
             scale = 1.0 / math.sqrt(32768)
             g4[div(row, 2), core] = (jnp.concatenate(lines, axis=0) * scale).astype(BF16)
-        if stage_id < 2:
-            gw_start(stage_id + 1)
-        else:
-            for d in range(2, 16, 2):
-                gw_hop(3, d, False).start()
+        gw_start(stage_id + 1)
 
     def gw_across(receive):
         side = g4.at[:, 1 - core if receive else core]
         return remote(side, side, gw_send.at[3, 1], gw_recv.at[3, 1], partner)
 
-    gw_start(0)
     for h in range(PARTS):
         for way, sign, device in ways:
             z_first(h, way, sign, device).wait_send()
             for step in range(1, 4):
                 z_hop(h, way, step, device).wait_send()
         y_hop(h).wait_send()
-    for h in range(AG_PARTS):
-        ag_side(h, rem(team + 8, 16)).wait_recv()
-        for way, sign, device in ways:
-            ag_hop(1, way, 1, h, device).start()
-    for step in range(2, 5):
+    for tick in range(2, 6):
         for rel in range(2):
+            step = tick - rel
+            if step > 4:
+                continue
             for h in range(AG_PARTS):
+                if step == 1:
+                    ag_side(h, rem(team + 8, 16)).wait_recv()
                 for way, sign, device in ways:
-                    ag_wait(step - 1, way, rel, h, device)
+                    if step > 1:
+                        ag_wait(step - 1, way, rel, h, device)
                     if step < 4 or rel == way:
                         ag_hop(step, way, rel, h, device).start()
-        if step == 3:
+        if tick == 2:
+            gw_chip()
+        elif tick == 4:
             gw_stage(0)
     for rel in range(2):
         for h in range(AG_PARTS):
@@ -595,12 +607,10 @@
                     if step < 4 or rel == way:
                         ag_hop(step, way, rel, h, device).wait_send()
 
-    def sent(d, carry):
-        for stage_id in range(3):
+    gw_pair().wait_send()
+    for stage_id in range(3):
+        for d in peers(stage_id):
             gw_hop(stage_id, d, False).wait_send()
-        return carry
-
-    lax.fori_loop(1, 16, sent, 0)
     for h in range(PARTS):
         for way, sign, device in x_ways:
             x_first(h, way, device).wait_recv()
@@ -622,8 +632,7 @@
         bs[h] = sums[1].astype(BF16)
         b_hop(h).start()
         keep[:, h * WIDE : (h + 1) * WIDE] = sums[0]
-    for d in range(2, 16, 2):
-        gw_hop(3, d, True).wait_recv()
+    gw_arrive(3)
     gw_across(False).start()
     for h in range(PARTS):
         b_hop(h).wait_recv()
@@ -633,7 +642,7 @@
 
     gw_across(True).wait_recv()
     gw_out[...] = g4[...].reshape(16, 32, 512)
-    for d in range(2, 16, 2):
+    for d in peers(3):
         gw_hop(3, d, False).wait_send()
     gw_across(False).wait_send()
     for h in range(PARTS):
@@ -671,9 +680,12 @@
             pltpu.VMEM(half, BF16),
             pltpu.VMEM((128, 512), F32),
             pltpu.VMEM((16, 128, 512), BF16),
-            pltpu.VMEM((16, 32, 512), F32),
-            pltpu.VMEM((16, 32, 512), BF16),
-            pltpu.VMEM((16, 32, 512), BF16),
+            pltpu.VMEM((8, 2, 32, 512), F32),
+            pltpu.VMEM((8, 2, 32, 512), BF16),
+            pltpu.VMEM((8, 32, 512), BF16),
+            pltpu.VMEM((8, 32, 512), F32),
+            pltpu.VMEM((8, 32, 512), BF16),
+            pltpu.VMEM((8, 32, 512), BF16),
             pltpu.VMEM((16, 8, 128), F32),
             pltpu.VMEM((16, 8, 128), F32),
             pltpu.VMEM((16, 8, 128), F32),

time: 123 us -> 120 us (0.976)
  Pallas kernels: 116 us -> 113 us
    pallas_call x1, Pallas kernels: 116 us -> 113 us  [per_device(): pl.pallas_call(layer_kernel, out_shape=(jax.ShapeDtypeStruct((128, 512),...]
where the time goes in v4:
time: 120 us
  Pallas kernels  113 us (94%)
  local copies, waits for them, and re-layouts  3.13 us (3%)
  other arithmetic  2.15 us (2%)
  between operations  1.29 us (1%)
    pallas_call x1, Pallas kernels, per_device(): pl.pallas_call(layer_kernel, out_shape=(jax.ShapeDtypeStruct((128, 512),...  113 us
    unnamed x2, local copies, waits for them, and re-layouts  3.13 us

profile of v4, /device:TPU:1, one launch (start us, length us, event | category | flops | bytes accessed | tf_op | source)
XLA Modules:
  0.0 119.8 jit_solution(7146944789775156323)
XLA Ops:
  1.3 113.2 %layer.1 = (bf16[128,512]{1,0:T(8,128)(2,1)}, bf16[16,32,512]{2,1,0:T(8,128)(2,1)}, bf16[128,512]{1,0:T(8,128)(2,1)}) custom-call(bf16[2048,512]{1,0:T(8,128)(2,1)} %feat.1, bf16[512,512]{1,0:T(8,128)(2,1)} %weight.1, bf16[8,512]{1,0:T(8,128)(2,1)} %table.1, s32[16,128]{1,0:T(8,128)} %bitcast.13, s32[16,128]{1,0:T(8,128)} %bitcast.14, ...), custom_call_target="tpu_custom_call" | custom-call | tf_op jit(solution)/shard_map/layer/pallas_call | solution.py:663
  114.5 2.1 %bitcast_convert_fusion = f32[512,512]{1,0:T(8,128)} fusion(bf16[16,32,512]{2,1,0:T(8,128)(2,1)} %get-tuple-element.7), kind=kLoop, calls=%fused_computation | loop fusion | flops 262144 | bytes 1572864 | tf_op jit(solution)/shard_map/convert_element_type | solution.py:732
  116.6 1.6 %copy.15 = bf16[128,512]{1,0:T(8,128)(2,1)} copy(bf16[128,512]{1,0:T(8,128)(2,1)} %get-tuple-element.12) | data formatting | bytes 262144
  118.2 1.6 %copy.16 = bf16[1,128,512]{2,1,0:T(8,128)(2,1)} copy(bf16[1,128,512]{2,1,0:T(8,128)(2,1)} %bitcast.12) | data formatting | bytes 262144

commit v5 on v4

--- a/solution.py
+++ b/solution.py
@@ -172,8 +172,6 @@
         lax.fori_loop(0, pieces, begin, 0)
 
     slots[16] = jnp.zeros((128, 512), F32)
-    for k in range(16):
-        vt[k] = vals[k].T
 
     pl.semaphore_wait(barrier, 31)
 
@@ -322,6 +320,9 @@
     for h in range(PARTS):
         for way, sign, device in ways:
             z_first(h, way, sign, device).start()
+
+    for k in range(16):
+        vt[k] = vals[k].T
 
     @pl.when(lead)
     def _():

time: 120 us -> 120 us (level)
  no operation moved by 1% of the time
where the time goes in v5:
time: 120 us
  Pallas kernels  113 us (94%)
  local copies, waits for them, and re-layouts  3.13 us (3%)
  other arithmetic  2.15 us (2%)
  between operations  1.29 us (1%)
    pallas_call x1, Pallas kernels, per_device(): pl.pallas_call(layer_kernel, out_shape=(jax.ShapeDtypeStruct((128, 512),...  113 us
    unnamed x2, local copies, waits for them, and re-layouts  3.13 us

profile of v5, /device:TPU:1, one launch (start us, length us, event | category | flops | bytes accessed | tf_op | source)
XLA Modules:
  0.0 119.8 jit_solution(17318378259806045162)
XLA Ops:
  1.3 113.2 %layer.1 = (bf16[128,512]{1,0:T(8,128)(2,1)}, bf16[16,32,512]{2,1,0:T(8,128)(2,1)}, bf16[128,512]{1,0:T(8,128)(2,1)}) custom-call(bf16[2048,512]{1,0:T(8,128)(2,1)} %feat.1, bf16[512,512]{1,0:T(8,128)(2,1)} %weight.1, bf16[8,512]{1,0:T(8,128)(2,1)} %table.1, s32[16,128]{1,0:T(8,128)} %bitcast.13, s32[16,128]{1,0:T(8,128)} %bitcast.14, ...), custom_call_target="tpu_custom_call" | custom-call | tf_op jit(solution)/shard_map/layer/pallas_call | solution.py:664
  114.5 2.1 %bitcast_convert_fusion = f32[512,512]{1,0:T(8,128)} fusion(bf16[16,32,512]{2,1,0:T(8,128)(2,1)} %get-tuple-element.7), kind=kLoop, calls=%fused_computation | loop fusion | flops 262144 | bytes 1572864 | tf_op jit(solution)/shard_map/convert_element_type | solution.py:733
  116.6 1.6 %copy.15 = bf16[128,512]{1,0:T(8,128)(2,1)} copy(bf16[128,512]{1,0:T(8,128)(2,1)} %get-tuple-element.12) | data formatting | bytes 262144
  118.2 1.6 %copy.16 = bf16[1,128,512]{2,1,0:T(8,128)(2,1)} copy(bf16[1,128,512]{2,1,0:T(8,128)(2,1)} %bitcast.12) | data formatting | bytes 262144
